TPU v7x, 32 devices: a whole 2x2x4 slice. The times are simulated.
32 devices in a mesh: groups: 2 (over x), wide: 16 (over z, y, core).
Axes of the slice: x: 2, y: 2, z: 4, core: 2. Of those that a mesh axis runs over, the one named last changes fastest.
Arguments:
- iterate: float32 [8192, 128], P(('groups', 'wide')), parts along dimension 0, may hold values from -6 to 6
- rhs: float32 [8192, 128], P(('groups', 'wide')), parts along dimension 0, may hold values from -6 to 6
- schur: float32 [32, 384, 384], P(('groups', 'wide')), parts along dimension 0
- near_block: float32 [8192, 256], P(('groups', 'wide')), parts along dimension 0
- u_basis: float32 [32, 32, 4096], P('groups', None, 'wide'), parts along dimension 0, may hold values from -0.375 to 0.375
- v_basis: float32 [32, 32, 4096], P('groups', None, 'wide'), parts along dimension 0, may hold values from -0.375 to 0.375
- tile_rank: int32 [32, 16], P('groups', 'wide'), parts along dimension 0, may hold values from 1 to 32
- send_rows: int32 [32, 3, 128], P(('groups', 'wide')), parts along dimension 0, may hold values from 0 to 255
- send_count: int32 [32, 3], P(('groups', 'wide')), parts along dimension 0, may hold values from 0 to 128, as said below
- precond: float32 [8192], P(('groups', 'wide')), parts along dimension 0, may hold values from 0.1 to 1
Outputs:
- updated: float32 [8192, 128], P(('groups', 'wide')), parts along dimension 0
- residual: float32 [8192, 128], P(('groups', 'wide')), parts along dimension 0
There are 2 independent parts, one for each index of `groups`. A program takes and returns all parts, laid end to end along the dimension named above; each array names one. Nothing has to cross between parts.
Inputs may be any that keep to these rules, and one draw needn't show every extreme that they name: send_count[p, 0] is 0 for p = 0 and send_count[p, 2] is 0 for p = 15; a block is full in every draw.
All inputs are finite; a program needn't handle non-finite values.
Results may differ from a plain program's by a relative error of at most 0.0003.
Values sent between devices are 32-bit elements; how exact they have to be, the bound alone decides.
A program may use at most 64 MiB of HBM per device.

v0:
```python
import jax
import jax.numpy as jnp
from jax import lax
from jax.sharding import PartitionSpec as P


def shifted(block, axis, distance):
    devices = range(lax.axis_size(axis))
    route = [(i - distance, i) for i in devices if i - distance in devices]
    return lax.ppermute(block, axis, route)


def body(
    iterate, rhs, schur, near_block, u_basis, v_basis, tile_rank, send_rows, send_count, precond
):
    highest = lax.Precision.HIGHEST
    rows_here = iterate.shape[0]
    loads = iterate.shape[1]
    face_rows = send_rows.shape[2]
    slots_all = 3 * face_rows
    tiles = u_basis.shape[0]
    rank_top = u_basis.shape[1]
    rows_local = jnp.arange(rows_here, dtype=jnp.int32)
    slot_ids = jnp.arange(face_rows, dtype=jnp.int32)
    valid = (slot_ids[None, :] < send_count[0][:, None]).reshape(slots_all)
    flat_rows = send_rows[0].reshape(slots_all)
    select = ((flat_rows[:, None] == rows_local[None, :]) & valid[:, None]).astype(jnp.float32)
    outgoing = jnp.dot(select, iterate, precision=highest, preferred_element_type=jnp.float32)
    outgoing = outgoing.reshape(3, face_rows, loads)
    pieces = [None, outgoing[1], None]
    for slot, offset in ((0, -1), (2, 1)):
        pieces[slot] = shifted(outgoing[slot], "wide", offset)
    incoming = jnp.stack(pieces, axis=0)
    forces = jnp.dot(
        schur[0],
        incoming.reshape(slots_all, loads),
        precision=highest,
        preferred_element_type=jnp.float32,
    ).reshape(3, face_rows, loads)
    pieces = [None, forces[1], None]
    for slot, offset in ((0, -1), (2, 1)):
        pieces[slot] = shifted(forces[slot], "wide", -offset)
    returned = jnp.stack(pieces, axis=0)
    fem = lax.dot_general(
        select,
        returned.reshape(slots_all, loads),
        (((0,), (0,)), ((), ())),
        precision=highest,
        preferred_element_type=jnp.float32,
    )
    coeff = jnp.dot(
        v_basis.reshape(tiles * rank_top, rows_here),
        iterate,
        precision=highest,
        preferred_element_type=jnp.float32,
    ).reshape(tiles, rank_top, loads)
    keep = (jnp.arange(rank_top, dtype=jnp.int32)[None, :] < tile_rank).astype(jnp.float32)
    coeff = coeff * keep[:, :, None]
    u_flat = u_basis.reshape(tiles * rank_top, rows_here)
    gathered = lax.all_to_all(coeff, "wide", split_axis=0, concat_axis=0, tiled=True)
    far = lax.dot_general(
        u_flat,
        gathered.reshape(tiles * rank_top, gathered.shape[2]),
        (((0,), (0,)), ((), ())),
        precision=highest,
        preferred_element_type=jnp.float32,
    )
    near = jnp.dot(near_block, iterate, precision=highest, preferred_element_type=jnp.float32)
    residual = rhs - (fem + (far + near))
    updated = iterate + precond[:, None] * residual
    return (updated, residual)


def solution(mesh):
    in_specs = (
        P(("groups", "wide"), None),
        P(("groups", "wide"), None),
        P(("groups", "wide"), None, None),
        P(("groups", "wide"), None),
        P("groups", None, "wide"),
        P("groups", None, "wide"),
        P("groups", "wide"),
        P(("groups", "wide"), None, None),
        P(("groups", "wide"), None),
        P(("groups", "wide")),
    )
    out_specs = (P(("groups", "wide"), None), P(("groups", "wide"), None))
    return jax.shard_map(body, mesh=mesh, in_specs=in_specs, out_specs=out_specs, check_vma=False)
```

profile of v0, /device:TPU:1, one launch (start us, length us, event | category | flops | bytes accessed | tf_op | source)
XLA Modules:
  0.0 29.8 jit_solution(5099675021365020917)
XLA Ops:
  0.6 0.0 copy-start
  0.6 0.0 copy-start.9
  0.7 0.0 copy-start.6
  0.7 0.0 copy-start.2
  0.7 0.7 %copy-done.9 = s32[1,3]{1,0:T(1,128)S(1)} copy-done((s32[1,3]{1,0:T(1,128)S(1)}, s32[1,3]{1,0:T(1,128)}, u32[]{:S(2)}) %copy-start.9) | copy-done | bytes 36
  1.4 0.1 fusion.14
  1.4 0.0 copy-done.6
  1.5 1.3 %fusion.6 = f32[384,128]{1,0:T(8,128)S(1)} fusion(f32[256,128]{1,0:T(8,128)} %param.10, s32[384]{0:T(512)S(1)} %bitcast.41, pred[384]{0:T(512)(128)(4,1)S(1)} %fusion.14), kind=kOutput, calls=%fused_computation.10 | convolution fusion | flops 151191552 | bytes 329600 | tf_op jit(solution)/shard_map/dot_general | solution.py:28
  2.8 0.0 copy-start.1
  2.8 2.1 %collective-permute-start = (f32[128,128]{1,0:T(8,128)S(1)}, f32[128,128]{1,0:T(8,128)S(1)}, u32[]{:S(2)}, u32[]{:S(2)}) collective-permute-start(f32[128,128]{1,0:T(8,128)S(1)} %get-tuple-element.5), channel_id=1, source_target_pairs={{1,0},{2,1},{3,2},{4,3},{5,4},{6,5},{7,6},{8,7},{9,8},{10,9},{11,1... | collective-permute-start | bytes 196616 | tf_op jit(solution)/shard_map/ppermute | solution.py:10
  4.9 0.0 copy-start.8
  4.9 4.5 %collective-permute-start.1 = (f32[128,128]{1,0:T(8,128)S(1)}, f32[128,128]{1,0:T(8,128)S(1)}, u32[]{:S(2)}, u32[]{:S(2)}) collective-permute-start(f32[128,128]{1,0:T(8,128)S(1)} %get-tuple-element.6), channel_id=1, source_target_pairs={{0,1},{1,2},{2,3},{3,4},{4,5},{5,6},{6,7},{7,8},{8,9},{9,10},{10,1... | collective-permute-start | bytes 196616 | tf_op jit(solution)/shard_map/ppermute | solution.py:10
  9.4 0.0 copy-done.8
  9.4 0.1 fusion.13
  9.5 0.0 copy-done.2
  9.5 0.0 copy-done.1
  9.5 1.3 %convolution_multiply_fusion = f32[16,32,128]{2,1,0:T(8,128)} fusion(f32[16,32,256]{2,1,0:T(8,128)S(1)} %copy-done.2, f32[256,128]{1,0:T(8,128)S(1)} %copy-done.1, f32[16,32]{1,0:T(8,128)S(1)} %fusion.13), kind=kOutput, calls=%fused_computation | convolution fusion | flops 201392128 | bytes 919552 | tf_op jit(solution)/shard_map/dot_general | solution.py:51
  10.8 5.8 %all-to-all-start = ((f32[16,32,128]{2,1,0:T(8,128)}), f32[16,32,128]{2,1,0:T(8,128)S(1)}, u32[]{:S(2)}, u32[]{:S(2)}) async-start(f32[16,32,128]{2,1,0:T(8,128)} %convolution_multiply_fusion), calls=%async_computation | async-start | bytes 524288 | tf_op jit(solution)/shard_map/all_to_all | solution.py:60
  16.6 0.0 collective-permute-done
  16.6 0.0 collective-permute-done.1
  16.6 0.0 copy-done
  16.6 0.8 %convolution_bitcast_fusion = f32[384,128]{0,1:T(8,128)S(1)} fusion(f32[384,128]{1,0:T(8,128)S(1)} %bitcast.36, f32[1,384,384]{2,1,0:T(8,128)S(1)} %copy-done), kind=kOutput, calls=%fused_computation.1 | convolution fusion | flops 226492416 | bytes 983040 | tf_op jit(solution)/shard_map/dot_general | solution.py:34
  17.5 3.5 %collective-permute-start.2 = (f32[128,128]{0,1:T(8,128)S(1)}, f32[128,128]{0,1:T(8,128)S(1)}, u32[]{:S(2)}, u32[]{:S(2)}) collective-permute-start(f32[128,128]{0,1:T(8,128)S(1)} %get-tuple-element.2), channel_id=1, source_target_pairs={{0,1},{1,2},{2,3},{3,4},{4,5},{5,6},{6,7},{7,8},{8,9},{9,10},{10,1... | collective-permute-start | bytes 196616 | tf_op jit(solution)/shard_map/ppermute | solution.py:10
  21.0 1.9 %collective-permute-start.3 = (f32[128,128]{0,1:T(8,128)S(1)}, f32[128,128]{0,1:T(8,128)S(1)}, u32[]{:S(2)}, u32[]{:S(2)}) collective-permute-start(f32[128,128]{0,1:T(8,128)S(1)} %get-tuple-element.3), channel_id=1, source_target_pairs={{1,0},{2,1},{3,2},{4,3},{5,4},{6,5},{7,6},{8,7},{9,8},{10,9},{11,1... | collective-permute-start | bytes 196616 | tf_op jit(solution)/shard_map/ppermute | solution.py:10
  22.9 0.0 collective-permute-done.2
  23.0 3.7 %collective-permute-done.3 = f32[128,128]{0,1:T(8,128)S(1)} collective-permute-done((f32[128,128]{0,1:T(8,128)S(1)}, f32[128,128]{0,1:T(8,128)S(1)}, u32[]{:S(2)}, u32[]{:S(2)}) %collective-permute-start.3) | collective-permute-done | bytes 65568 | tf_op jit(solution)/shard_map/ppermute | solution.py:10
  26.7 0.0 copy-start.3
  26.7 0.1 copy.13
  26.8 0.6 %fusion.4 = f32[256,128]{1,0:T(8,128)S(1)} fusion(f32[384,128]{1,0:T(8,128)S(1)} %bitcast.35, s32[384]{0:T(512)S(1)} %bitcast.42, pred[384]{0:T(512)(128)(4,1)S(1)} %fusion.14), kind=kOutput, calls=%fused_computation.9 | convolution fusion | flops 151191552 | bytes 329600 | tf_op jit(solution)/shard_map/dot_general | solution.py:44
  27.5 0.0 copy-start.4
  27.5 0.0 copy-start.5
  27.5 0.0 copy-start.7
  27.5 0.0 all-to-all-done
  27.5 0.2 copy-done.3
  27.7 1.0 %convolution_bitcast_fusion.1 = f32[256,128]{1,0:T(8,128)S(1)} fusion(f32[16,32,128]{2,1,0:T(8,128)S(1)} %all-to-all-done, f32[16,32,256]{2,1,0:T(8,128)S(1)} %copy-done.3), kind=kOutput, calls=%fused_computation.5 | convolution fusion | flops 201326592 | bytes 917504 | tf_op jit(solution)/shard_map/dot_general | solution.py:61
  28.7 0.0 copy-done.4
  28.7 0.0 copy-done.5
  28.7 0.0 copy-done.7
  28.8 1.1 %multiply_add_fusion = (f32[256,128]{1,0:T(8,128)}, f32[256,128]{1,0:T(8,128)}) fusion(f32[256,128]{1,0:T(8,128)S(1)} %copy-done.1, f32[256]{0:T(256)S(1)} %copy-done.7, f32[256,128]{1,0:T(8,128)S(1)} %copy-done.5, f32[256,128]{1,0:T(8,128)S(1)} %fusion.4, f32[256,128]{1,0:T(8,128)S(1)} %convolution_bitcast_fusion.1, f32[256,256]{1,0:T(8,128)S(1)} %copy-done.4), kind=kOutput, calls=%fused_computation.18 | convolution fusion | flops 100827136 | bytes 1049600 | tf_op jit(solution)/shard_map/dot_general | solution.py:68
  (5 shorter events, 0.1 us)
Async XLA Ops:
  0.6 16.0 %copy-start = (f32[1,384,384]{2,1,0:T(8,128)S(1)}, f32[1,384,384]{2,1,0:T(8,128)}, u32[]{:S(2)}) copy-start(f32[1,384,384]{2,1,0:T(8,128)} %param.12) | copy-start | bytes 1769476
  0.6 0.7 %copy-start.9 = (s32[1,3]{1,0:T(1,128)S(1)}, s32[1,3]{1,0:T(1,128)}, u32[]{:S(2)}) copy-start(s32[1,3]{1,0:T(1,128)} %param.18) | copy-start | bytes 40
  0.7 0.8 %copy-start.6 = (s32[1,3,128]{2,0,1:T(1,128)S(1)}, s32[1,3,128]{2,0,1:T(1,128)}, u32[]{:S(2)}) copy-start(s32[1,3,128]{2,0,1:T(1,128)} %param.17) | copy-start | bytes 4612
  0.7 8.8 %copy-start.2 = (f32[16,32,256]{2,1,0:T(8,128)S(1)}, f32[16,32,256]{2,1,0:T(8,128)}, u32[]{:S(2)}) copy-start(f32[16,32,256]{2,1,0:T(8,128)} %param.15) | copy-start | bytes 1572868
  2.8 6.7 %copy-start.1 = (f32[256,128]{1,0:T(8,128)S(1)}, f32[256,128]{1,0:T(8,128)}, u32[]{:S(2)}) copy-start(f32[256,128]{1,0:T(8,128)} %param.10) | copy-start | bytes 393220
  2.8 13.8 %collective-permute-start = (f32[128,128]{1,0:T(8,128)S(1)}, f32[128,128]{1,0:T(8,128)S(1)}, u32[]{:S(2)}, u32[]{:S(2)}) collective-permute-start(f32[128,128]{1,0:T(8,128)S(1)} %get-tuple-element.5), channel_id=1, source_target_pairs={{1,0},{2,1},{3,2},{4,3},{5,4},{6,5},{7,6},{8,7},{9,8},{10,9},{11,1... | collective-permute-start | bytes 196616 | tf_op jit(solution)/shard_map/ppermute | solution.py:10
  4.9 4.5 %copy-start.8 = (s32[16,1]{0,1:T(1,128)S(1)}, s32[16,1]{0,1:T(1,128)}, u32[]{:S(2)}) copy-start(s32[16,1]{0,1:T(1,128)} %param.16) | copy-start | bytes 196
  4.9 11.7 %collective-permute-start.1 = (f32[128,128]{1,0:T(8,128)S(1)}, f32[128,128]{1,0:T(8,128)S(1)}, u32[]{:S(2)}, u32[]{:S(2)}) collective-permute-start(f32[128,128]{1,0:T(8,128)S(1)} %get-tuple-element.6), channel_id=1, source_target_pairs={{0,1},{1,2},{2,3},{3,4},{4,5},{5,6},{6,7},{7,8},{8,9},{9,10},{10,1... | collective-permute-start | bytes 196616 | tf_op jit(solution)/shard_map/ppermute | solution.py:10
  10.8 16.7 %all-to-all-start = ((f32[16,32,128]{2,1,0:T(8,128)}), f32[16,32,128]{2,1,0:T(8,128)S(1)}, u32[]{:S(2)}, u32[]{:S(2)}) async-start(f32[16,32,128]{2,1,0:T(8,128)} %convolution_multiply_fusion), calls=%async_computation | async-start | bytes 524288 | tf_op jit(solution)/shard_map/all_to_all | solution.py:60
  17.5 5.5 %collective-permute-start.2 = (f32[128,128]{0,1:T(8,128)S(1)}, f32[128,128]{0,1:T(8,128)S(1)}, u32[]{:S(2)}, u32[]{:S(2)}) collective-permute-start(f32[128,128]{0,1:T(8,128)S(1)} %get-tuple-element.2), channel_id=1, source_target_pairs={{0,1},{1,2},{2,3},{3,4},{4,5},{5,6},{6,7},{7,8},{8,9},{9,10},{10,1... | collective-permute-start | bytes 196616 | tf_op jit(solution)/shard_map/ppermute | solution.py:10
  21.0 5.7 %collective-permute-start.3 = (f32[128,128]{0,1:T(8,128)S(1)}, f32[128,128]{0,1:T(8,128)S(1)}, u32[]{:S(2)}, u32[]{:S(2)}) collective-permute-start(f32[128,128]{0,1:T(8,128)S(1)} %get-tuple-element.3), channel_id=1, source_target_pairs={{1,0},{2,1},{3,2},{4,3},{5,4},{6,5},{7,6},{8,7},{9,8},{10,9},{11,1... | collective-permute-start | bytes 196616 | tf_op jit(solution)/shard_map/ppermute | solution.py:10
  26.7 1.0 %copy-start.3 = (f32[16,32,256]{2,1,0:T(8,128)S(1)}, f32[16,32,256]{2,1,0:T(8,128)}, u32[]{:S(2)}) copy-start(f32[16,32,256]{2,1,0:T(8,128)} %param.14) | copy-start | bytes 1572868
  27.5 1.2 %copy-start.4 = (f32[256,256]{1,0:T(8,128)S(1)}, f32[256,256]{1,0:T(8,128)}, u32[]{:S(2)}) copy-start(f32[256,256]{1,0:T(8,128)} %param.13) | copy-start | bytes 786436
  27.5 1.2 %copy-start.5 = (f32[256,128]{1,0:T(8,128)S(1)}, f32[256,128]{1,0:T(8,128)}, u32[]{:S(2)}) copy-start(f32[256,128]{1,0:T(8,128)} %param.11) | copy-start | bytes 393220
  27.5 1.2 %copy-start.7 = (f32[256]{0:T(256)S(1)}, f32[256]{0:T(256)}, u32[]{:S(2)}) copy-start(f32[256]{0:T(256)} %param.19) | copy-start | bytes 3076
where the time goes:
time: 30.2 us; the launch traced here: 29.8 us
  starting transfers between devices  17.8 us (59%)
  matrix products  6.11 us (20%)
  waiting for transfers between devices  3.74 us (12%)
  local copies, waits for them, and re-layouts  1.1 us (4%)
  between operations  0.86 us (3%)
    ppermute x4, starting transfers between devices, shifted(): return lax.ppermute(block, axis, route)  12 us
    all_to_all x1, starting transfers between devices, body(): lax.all_to_all(coeff, 'wide', split_axis=0, concat_axis=0, tiled=True)  5.78 us
    ppermute x4, waiting for transfers between devices, shifted(): return lax.ppermute(block, axis, route)  3.74 us
    dot_general x1, matrix products, body(): jnp.dot(select, iterate, precision=highest, preferred_element_type=jnp.fl...  1.3 us
    dot_general x1, matrix products, body(): jnp.dot(v_basis.reshape(tiles * rank_top, rows_here), iterate, precision=...  1.29 us
    dot_general x1, matrix products, body(): jnp.dot(near_block, iterate, precision=highest, preferred_element_type=jn...  1.08 us
    dot_general x1, matrix products, body(): lax.dot_general(u_flat, gathered.reshape(tiles * rank_top, gathered.shape...  0.99 us
    unnamed x20, local copies, waits for them, and re-layouts  0.94 us
  transfers between devices with their start and end apart: 5, of which 1 were waited for; matrix products, arithmetic and copies ran while one was open for 10% of the time, Pallas kernels for 0%

commit v1 on v0

v1 whole, which is shorter than its diff:
```python
import functools
import math

import jax
import jax.numpy as jnp
from jax import lax
from jax.experimental import pallas as pl
from jax.experimental.pallas import tpu as pltpu
from jax.sharding import PartitionSpec as P

MESH = pl.DeviceIdType.MESH
F32 = jnp.float32
BF16 = jnp.bfloat16


def halves(x):
    high = x.astype(BF16)
    low = (x - high.astype(F32)).astype(BF16)
    return high, low


def mm(a, b):
    return jnp.dot(a, b, preferred_element_type=F32)


def pair(x):
    high, low = halves(x)
    return jnp.concatenate([high, low], axis=1), high


def fold(p):
    width = p.shape[1] // 2
    return p[:, :width] + p[:, width:]


def product(a_high, a_low, b_both, b_high):
    return fold(mm(a_high, b_both)) + mm(a_low, b_high)


def kernel(
    n,
    iterate_hbm, schur_hbm, near_hbm, u_hbm, v_hbm, rank_hbm, rows_hbm, count_hbm,
    out_ref,
    iterate, schur, near, u, v, rank, rows, count,
    out_face, in_face, out_force, in_force, sent, gathered,
    u_high, u_low, s_high, s_low,
    load_sem, face_send, face_recv, force_send, force_recv, send_sem, recv_sem,
):
    me = lax.axis_index("wide")
    loads = iterate.shape[1]
    face = rows.shape[2]
    rank_top = v.shape[1]
    rows_here = iterate.shape[0]
    power = n & (n - 1) == 0
    bits = [1 << b for b in range(n.bit_length()) if 1 << b < n]
    flips = [bit * (1 - 2 * lax.rem(lax.div(me, bit), 2)) for bit in bits]

    def to_of(k):
        if power:
            return me + sum(flip for bit, flip in zip(bits, flips) if k & bit)
        return lax.rem(me + k, n)

    def from_of(k):
        return to_of(k) if power else lax.rem(me - k + n, n)

    barrier = pltpu.get_barrier_semaphore()
    for k in range(n - 1, 0, -1):
        pl.semaphore_signal(barrier, inc=1, device_id={"wide": to_of(k)}, device_id_type=MESH)

    names = {}
    order = (
        ("rows", rows_hbm, rows), ("count", count_hbm, count), ("iterate", iterate_hbm, iterate),
        ("rank", rank_hbm, rank), ("v", v_hbm, v), ("schur", schur_hbm, schur),
        ("u", u_hbm, u), ("near", near_hbm, near),
    )
    for at, (name, source, target) in enumerate(order):
        names[name] = pltpu.make_async_copy(source, target, load_sem.at[at])
        names[name].start()

    @pl.when(me == 0)
    def _():
        in_face[2] = jnp.zeros_like(in_face[2])
        in_force[0] = jnp.zeros_like(in_force[0])

    @pl.when(me == n - 1)
    def _():
        in_face[0] = jnp.zeros_like(in_face[0])
        in_force[2] = jnp.zeros_like(in_force[2])

    names["rows"].wait()
    names["count"].wait()
    slot_ids = lax.broadcasted_iota(jnp.int32, (1, face), 1)
    row_of = []
    for o in range(3):
        row_of.append(jnp.where(slot_ids < count[0, o], rows[o], -1))
    names["iterate"].wait()
    it_both, it_high = pair(iterate[...])
    lanes = lax.broadcasted_iota(jnp.int32, (face, rows_here), 1)
    for o in (0, 2, 1):
        column = jnp.broadcast_to(row_of[o].astype(F32), (face, face)).T[:, :1].astype(jnp.int32)
        select = (column == lanes).astype(F32).astype(BF16)
        picked = fold(mm(select, it_both))
        if o == 1:
            in_face[1] = picked
        else:
            out_face[o // 2] = picked

    names["rank"].wait()
    names["v"].wait()
    group = math.gcd(n, max(1, 128 // rank_top))
    rank_ids = lax.broadcasted_iota(jnp.int32, (rank_top, loads), 0)
    for first in range(n - group, -1, -group):
        block = jnp.concatenate([v[to_of(first + g)] for g in range(group)], axis=0)
        v_high, v_low = halves(block)
        coeff = product(v_high, v_low, it_both, it_high)
        for g in range(group):
            part = coeff[g * rank_top : (g + 1) * rank_top]
            part = jnp.where(rank_ids < rank[0, to_of(first + g)], part, 0.0)
            if first + g == 0:
                gathered[0] = part
            else:
                sent[first + g] = part

    pl.semaphore_wait(barrier, n - 1)

    def face_copy(o, source, target, send, recv, peer):
        return pltpu.make_async_remote_copy(
            src_ref=source, dst_ref=target, send_sem=send.at[o // 2], recv_sem=recv.at[o // 2],
            device_id={"wide": peer}, device_id_type=MESH,
        )

    below, above = lax.rem(me + n - 1, n), lax.rem(me + 1, n)
    faces = {
        0: face_copy(0, out_face.at[0], in_face.at[0], face_send, face_recv, below),
        2: face_copy(2, out_face.at[1], in_face.at[2], face_send, face_recv, above),
    }
    returns = {
        0: face_copy(0, out_force.at[0], in_force.at[0], force_send, force_recv, above),
        2: face_copy(2, out_force.at[1], in_force.at[2], force_send, force_recv, below),
    }
    has_below, has_above = me > 0, me < n - 1

    @pl.when(has_below)
    def _():
        faces[0].start()

    @pl.when(has_above)
    def _():
        faces[2].start()

    copies = {}
    for k in range(n - 1, 0, -1):
        copies[k] = pltpu.make_async_remote_copy(
            src_ref=sent.at[k], dst_ref=gathered.at[k], send_sem=send_sem.at[k], recv_sem=recv_sem.at[k],
            device_id={"wide": to_of(k)}, device_id_type=MESH,
        )
        copies[k].start()

    names["schur"].wait()
    high, low = halves(schur[0])
    s_high[...] = high
    s_low[...] = low
    mid = slice(face, 2 * face)
    b_both, b_high = pair(in_face[1])
    force = product(s_high[:, mid], s_low[:, mid], b_both, b_high)
    names["u"].wait()
    names["near"].wait()
    for first in range(0, n, group):
        block = jnp.concatenate([u[from_of(first + g)] for g in range(group)], axis=0).T
        high, low = halves(block)
        u_high[:, first * rank_top : (first + group) * rank_top] = high
        u_low[:, first * rank_top : (first + group) * rank_top] = low
    near_high, near_low = halves(near[...])
    out_ref[...] = product(near_high, near_low, it_both, it_high)

    @pl.when(has_above)
    def _():
        faces[0].wait_recv()

    @pl.when(has_below)
    def _():
        faces[2].wait_recv()

    for o in (0, 2):
        span = slice(o * face, (o + 1) * face)
        b_both, b_high = pair(in_face[o])
        force = force + product(s_high[:, span], s_low[:, span], b_both, b_high)
    out_force[0] = force[:face]
    out_force[1] = force[2 * face :]
    in_force[1] = force[mid]

    @pl.when(has_above)
    def _():
        returns[0].start()

    @pl.when(has_below)
    def _():
        returns[2].start()

    def far(first, size):
        for k in range(max(first, 1), first + size):
            copies[k].wait_recv()
        got = gathered[first : first + size].reshape(size * rank_top, loads)
        b_both, b_high = pair(got)
        span = slice(first * rank_top, (first + size) * rank_top)
        return product(u_high[:, span], u_low[:, span], b_both, b_high)

    chunk = math.gcd(n, 2 * group)
    for first in range(0, n - chunk, chunk):
        out_ref[...] += far(first, chunk)

    @pl.when(has_below)
    def _():
        returns[0].wait_recv()

    @pl.when(has_above)
    def _():
        returns[2].wait_recv()

    total = out_ref[...]
    place = lax.broadcasted_iota(jnp.int32, (rows_here, face), 0)
    for o in range(3):
        scatter = (place == row_of[o]).astype(F32).astype(BF16)
        b_both, _ = pair(in_force[o])
        total = total + fold(mm(scatter, b_both))
    total = total + far(n - chunk, chunk)
    out_ref[...] = total

    @pl.when(has_below)
    def _():
        faces[0].wait_send()
        returns[2].wait_send()

    @pl.when(has_above)
    def _():
        faces[2].wait_send()
        returns[0].wait_send()

    for k in range(1, n):
        copies[k].wait_send()


def body(
    iterate, rhs, schur, near_block, u_basis, v_basis, tile_rank, send_rows, send_count, precond
):
    n = lax.axis_size("wide")
    rows_here, loads = iterate.shape
    face = send_rows.shape[2]
    tiles, rank_top, _ = u_basis.shape
    tile_rank = tile_rank.reshape(1, tiles)
    send_rows = send_rows.reshape(3, 1, face)
    dma = pltpu.SemaphoreType.DMA
    applied = pl.pallas_call(
        functools.partial(kernel, n),
        out_shape=pltpu.VMEM((rows_here, loads), F32),
        in_specs=[pl.BlockSpec(memory_space=pl.ANY)] * 8,
        out_specs=pl.BlockSpec(memory_space=pltpu.VMEM),
        scratch_shapes=[
            pltpu.VMEM(iterate.shape, F32),
            pltpu.VMEM(schur.shape, F32),
            pltpu.VMEM(near_block.shape, F32),
            pltpu.VMEM(u_basis.shape, F32),
            pltpu.VMEM(v_basis.shape, F32),
            pltpu.SMEM(tile_rank.shape, jnp.int32),
            pltpu.VMEM(send_rows.shape, jnp.int32),
            pltpu.SMEM(send_count.shape, jnp.int32),
            pltpu.VMEM((2, face, loads), F32),
            pltpu.VMEM((3, face, loads), F32),
            pltpu.VMEM((2, face, loads), F32),
            pltpu.VMEM((3, face, loads), F32),
            pltpu.VMEM((n, rank_top, loads), F32),
            pltpu.VMEM((n, rank_top, loads), F32),
            pltpu.VMEM((rows_here, tiles * rank_top), BF16),
            pltpu.VMEM((rows_here, tiles * rank_top), BF16),
            pltpu.VMEM(schur.shape[1:], BF16),
            pltpu.VMEM(schur.shape[1:], BF16),
            dma((8,)),
            dma((2,)),
            dma((2,)),
            dma((2,)),
            dma((2,)),
            dma((n,)),
            dma((n,)),
        ],
        compiler_params=pltpu.CompilerParams(collective_id=0, has_side_effects=True),
    )(iterate, schur, near_block, u_basis, v_basis, tile_rank, send_rows, send_count)
    residual = rhs - applied
    updated = iterate + precond[:, None] * residual
    return (updated, residual)


def solution(mesh):
    in_specs = (
        P(("groups", "wide"), None),
        P(("groups", "wide"), None),
        P(("groups", "wide"), None, None),
        P(("groups", "wide"), None),
        P("groups", None, "wide"),
        P("groups", None, "wide"),
        P("groups", "wide"),
        P(("groups", "wide"), None, None),
        P(("groups", "wide"), None),
        P(("groups", "wide")),
    )
    out_specs = (P(("groups", "wide"), None), P(("groups", "wide"), None))
    return jax.shard_map(body, mesh=mesh, in_specs=in_specs, out_specs=out_specs, check_vma=False)
```

time: 30.2 us -> 16.8 us (0.56)
  starting transfers between devices: 17.8 us -> 0 us
  Pallas kernels: 0 us -> 15.2 us
  matrix products: 6.11 us -> 0 us
  waiting for transfers between devices: 3.74 us -> 0 us
  local copies, waits for them, and re-layouts: 1.1 us -> 0.01 us
  other arithmetic: 0.19 us -> 0.76 us
    pallas_call x0 -> x1, Pallas kernels: none -> 15.2 us  [body(): pl.pallas_call(functools.partial(kernel, n), out_shape=pltpu.VMEM((rows_h...]
    ppermute x4 -> x0, starting transfers between devices: 12 us -> none  [shifted(): return lax.ppermute(block, axis, route)]
    dot_general x6 -> x0, matrix products: 6.11 us -> none  [the longest x1 1.3 us: body(): jnp.dot(select, iterate, precision=highest, preferred_element_type=jnp.fl...]
    all_to_all x1 -> x0, starting transfers between devices: 5.78 us -> none  [body(): lax.all_to_all(coeff, 'wide', split_axis=0, concat_axis=0, tiled=True)]
    ppermute x4 -> x0, waiting for transfers between devices: 3.74 us -> none  [shifted(): return lax.ppermute(block, axis, route)]
    unnamed x20 -> x6, local copies, waits for them, and re-layouts: 0.94 us -> 0.01 us
    add x0 -> x1, other arithmetic: none -> 0.76 us  [body(): updated = iterate + precond[:, None] * residual]
  transfers between devices with their start and end apart: 5 -> 0, of which waited for: 1 -> 0; matrix products, arithmetic and copies ran while one was open for 10% -> 0% of each run, Pallas kernels for 0% -> 0%
where the time goes in v1:
time: 16.8 us; the launch traced here: 16.6 us
  Pallas kernels  15.2 us (90%)
  other arithmetic  0.76 us (5%)
  between operations  0.69 us (4%)
    pallas_call x1, Pallas kernels, body(): pl.pallas_call(functools.partial(kernel, n), out_shape=pltpu.VMEM((rows_h...  15.2 us
    add x1, other arithmetic, body(): updated = iterate + precond[:, None] * residual  0.76 us

profile of v1, /device:TPU:1, one launch (start us, length us, event | category | flops | bytes accessed | tf_op | source)
XLA Modules:
  0.0 16.6 jit_solution(17504471947841330255)
XLA Ops:
  0.6 0.0 copy-start
  0.6 0.0 copy-start.1
  0.7 0.0 copy-start.2
  0.7 15.2 %shard_map.113 = f32[256,128]{1,0:T(8,128)S(1)} custom-call(f32[256,128]{1,0:T(8,128)} %iterate_hbm.1, f32[1,384,384]{2,1,0:T(8,128)} %schur_hbm.1, f32[256,256]{1,0:T(8,128)} %near_hbm.1, f32[16,32,256]{2,1,0:T(8,128)} %u_hbm.1, f32[16,32,256]{2,1,0:T(8,128)} %v_hbm.1, s32[1,16]{1,0:T(1,128)} %bitcast.3, s32[3,1,128]{2,1,0:T(1,128)} %bitcast.2, ...), custom_call_target="tpu_custom_call" | custom-call | tf_op jit(solution)/shard_map/pallas_call | solution.py:253
  15.8 0.0 copy-done
  15.8 0.0 copy-done.1
  15.8 0.0 copy-done.2
  15.9 0.8 %multiply_add_fusion = (f32[256,128]{1,0:T(8,128)}, f32[256,128]{1,0:T(8,128)}) fusion(f32[256,128]{1,0:T(8,128)S(1)} %copy-done, f32[256]{0:T(256)S(1)} %copy-done.2, f32[256,128]{1,0:T(8,128)S(1)} %copy-done.1, f32[256,128]{1,0:T(8,128)S(1)} %shard_map.113), kind=kLoop, calls=%fused_computation | loop fusion | flops 98304 | bytes 656384 | tf_op jit(solution)/shard_map/add | solution.py:288
Async XLA Ops:
  0.6 15.2 %copy-start = (f32[256,128]{1,0:T(8,128)S(1)}, f32[256,128]{1,0:T(8,128)}, u32[]{:S(2)}) copy-start(f32[256,128]{1,0:T(8,128)} %iterate_hbm.1) | copy-start | bytes 393220
  0.6 15.2 %copy-start.1 = (f32[256,128]{1,0:T(8,128)S(1)}, f32[256,128]{1,0:T(8,128)}, u32[]{:S(2)}) copy-start(f32[256,128]{1,0:T(8,128)} %param.11) | copy-start | bytes 393220
  0.7 15.2 %copy-start.2 = (f32[256]{0:T(256)S(1)}, f32[256]{0:T(256)}, u32[]{:S(2)}) copy-start(f32[256]{0:T(256)} %param.19) | copy-start | bytes 3076

commit v2 on v1

--- a/solution.py
+++ b/solution.py
@@ -8,6 +8,11 @@
 from jax.experimental.pallas import tpu as pltpu
 from jax.sharding import PartitionSpec as P
 
+EARLY = 2
+STRIDE = False
+FIRST = 0
+JOIN = 0
+TAIL = 1
 MESH = pl.DeviceIdType.MESH
 F32 = jnp.float32
 BF16 = jnp.bfloat16
@@ -67,16 +72,32 @@
     for k in range(n - 1, 0, -1):
         pl.semaphore_signal(barrier, inc=1, device_id={"wide": to_of(k)}, device_id_type=MESH)
 
+    group = math.gcd(n, max(1, 128 // rank_top))
+    if STRIDE:
+        groups = [[step + n // group * g for g in range(group - 1, -1, -1)] for step in range(n // group - 1, -1, -1)]
+    else:
+        groups = [[first + g for g in range(group - 1, -1, -1)] for first in range(n - group, -1, -group)]
+    slot_of = {k: at for at, k in enumerate(k for members in groups for k in members)}
+
     names = {}
-    order = (
-        ("rows", rows_hbm, rows), ("count", count_hbm, count), ("iterate", iterate_hbm, iterate),
-        ("rank", rank_hbm, rank), ("v", v_hbm, v), ("schur", schur_hbm, schur),
-        ("u", u_hbm, u), ("near", near_hbm, near),
-    )
-    for at, (name, source, target) in enumerate(order):
+    def load(name, at, source, target):
         names[name] = pltpu.make_async_copy(source, target, load_sem.at[at])
         names[name].start()
 
+    load("iterate", 0, iterate_hbm, iterate)
+    load("rank", 1, rank_hbm, rank)
+    for at, k in enumerate(slot_of):
+        if at < group:
+            load(k, 7 + at, v_hbm.at[to_of(k)], v.at[at])
+    load("rows", 2, rows_hbm, rows)
+    load("count", 3, count_hbm, count)
+    for at, k in enumerate(slot_of):
+        if at >= group:
+            load(k, 7 + at, v_hbm.at[to_of(k)], v.at[at])
+    load("schur", 4, schur_hbm, schur)
+    load("u", 5, u_hbm, u)
+    load("near", 6, near_hbm, near)
+
     @pl.when(me == 0)
     def _():
         in_face[2] = jnp.zeros_like(in_face[2])
@@ -86,6 +107,46 @@
     def _():
         in_face[0] = jnp.zeros_like(in_face[0])
         in_force[2] = jnp.zeros_like(in_force[2])
+
+    names["iterate"].wait()
+    it_both, it_high = pair(iterate[...])
+    rank_ids = lax.broadcasted_iota(jnp.int32, (rank_top, loads), 0)
+    copies = {
+        k: pltpu.make_async_remote_copy(
+            src_ref=sent.at[slot], dst_ref=gathered.at[slot], send_sem=send_sem.at[slot],
+            recv_sem=recv_sem.at[slot], device_id={"wide": to_of(k)}, device_id_type=MESH,
+        )
+        for k, slot in slot_of.items() if k > 0
+    }
+
+    def compress(members):
+        for k in members:
+            names[k].wait()
+        block = jnp.concatenate([v[slot_of[k]] for k in members], axis=0)
+        v_high, v_low = halves(block)
+        coeff = product(v_high, v_low, it_both, it_high)
+        for g, k in enumerate(members):
+            part = coeff[g * rank_top : (g + 1) * rank_top]
+            part = jnp.where(rank_ids < rank[0, to_of(k)], part, 0.0)
+            if k == 0:
+                gathered[slot_of[k]] = part
+            else:
+                sent[slot_of[k]] = part
+
+    def send(members):
+        for k in members:
+            if k > 0:
+                copies[k].start()
+
+    names["rank"].wait()
+    early = min(EARLY, len(groups))
+    for members in groups[:early]:
+        compress(members)
+
+    if FIRST:
+        pl.semaphore_wait(barrier, n - 1)
+        for members in groups[:early]:
+            send(members)
 
     names["rows"].wait()
     names["count"].wait()
@@ -93,8 +154,6 @@
     row_of = []
     for o in range(3):
         row_of.append(jnp.where(slot_ids < count[0, o], rows[o], -1))
-    names["iterate"].wait()
-    it_both, it_high = pair(iterate[...])
     lanes = lax.broadcasted_iota(jnp.int32, (face, rows_here), 1)
     for o in (0, 2, 1):
         column = jnp.broadcast_to(row_of[o].astype(F32), (face, face)).T[:, :1].astype(jnp.int32)
@@ -105,23 +164,8 @@
         else:
             out_face[o // 2] = picked
 
-    names["rank"].wait()
-    names["v"].wait()
-    group = math.gcd(n, max(1, 128 // rank_top))
-    rank_ids = lax.broadcasted_iota(jnp.int32, (rank_top, loads), 0)
-    for first in range(n - group, -1, -group):
-        block = jnp.concatenate([v[to_of(first + g)] for g in range(group)], axis=0)
-        v_high, v_low = halves(block)
-        coeff = product(v_high, v_low, it_both, it_high)
-        for g in range(group):
-            part = coeff[g * rank_top : (g + 1) * rank_top]
-            part = jnp.where(rank_ids < rank[0, to_of(first + g)], part, 0.0)
-            if first + g == 0:
-                gathered[0] = part
-            else:
-                sent[first + g] = part
-
-    pl.semaphore_wait(barrier, n - 1)
+    if not FIRST:
+        pl.semaphore_wait(barrier, n - 1)
 
     def face_copy(o, source, target, send, recv, peer):
         return pltpu.make_async_remote_copy(
@@ -148,13 +192,12 @@
     def _():
         faces[2].start()
 
-    copies = {}
-    for k in range(n - 1, 0, -1):
-        copies[k] = pltpu.make_async_remote_copy(
-            src_ref=sent.at[k], dst_ref=gathered.at[k], send_sem=send_sem.at[k], recv_sem=recv_sem.at[k],
-            device_id={"wide": to_of(k)}, device_id_type=MESH,
-        )
-        copies[k].start()
+    if not FIRST:
+        for members in groups[:early]:
+            send(members)
+    for members in groups[early:]:
+        compress(members)
+        send(members)
 
     names["schur"].wait()
     high, low = halves(schur[0])
@@ -165,11 +208,12 @@
     force = product(s_high[:, mid], s_low[:, mid], b_both, b_high)
     names["u"].wait()
     names["near"].wait()
-    for first in range(0, n, group):
-        block = jnp.concatenate([u[from_of(first + g)] for g in range(group)], axis=0).T
+    for at, members in enumerate(groups):
+        block = jnp.concatenate([u[from_of(k)] for k in members], axis=0).T
         high, low = halves(block)
-        u_high[:, first * rank_top : (first + group) * rank_top] = high
-        u_low[:, first * rank_top : (first + group) * rank_top] = low
+        span = slice(at * group * rank_top, (at + 1) * group * rank_top)
+        u_high[:, span] = high
+        u_low[:, span] = low
     near_high, near_low = halves(near[...])
     out_ref[...] = product(near_high, near_low, it_both, it_high)
 
@@ -198,16 +242,23 @@
         returns[2].start()
 
     def far(first, size):
-        for k in range(max(first, 1), first + size):
-            copies[k].wait_recv()
+        for k, slot in slot_of.items():
+            if k > 0 and first <= slot < first + size:
+                copies[k].wait_recv()
         got = gathered[first : first + size].reshape(size * rank_top, loads)
         b_both, b_high = pair(got)
         span = slice(first * rank_top, (first + size) * rank_top)
         return product(u_high[:, span], u_low[:, span], b_both, b_high)
 
-    chunk = math.gcd(n, 2 * group)
-    for first in range(0, n - chunk, chunk):
-        out_ref[...] += far(first, chunk)
+    spans = [(at * group, group) for at in range(len(groups))]
+    half = len(spans) // 2
+    spans = spans[half:][::-1] + spans[:half]
+    if JOIN and half > 1:
+        spans = spans[:-half] + [(at * group, 2 * group) for at in range(0, half - 1, 2)]
+        if half % 2:
+            spans = spans[:-1] + [((half - 1) * group, group), spans[-1]]
+    for first, size in spans[: len(spans) - TAIL]:
+        out_ref[...] += far(first, size)
 
     @pl.when(has_below)
     def _():
@@ -223,7 +274,8 @@
         scatter = (place == row_of[o]).astype(F32).astype(BF16)
         b_both, _ = pair(in_force[o])
         total = total + fold(mm(scatter, b_both))
-    total = total + far(n - chunk, chunk)
+    for first, size in spans[len(spans) - TAIL :]:
+        total = total + far(first, size)
     out_ref[...] = total
 
     @pl.when(has_below)
@@ -274,7 +326,7 @@
             pltpu.VMEM((rows_here, tiles * rank_top), BF16),
             pltpu.VMEM(schur.shape[1:], BF16),
             pltpu.VMEM(schur.shape[1:], BF16),
-            dma((8,)),
+            dma((7 + n,)),
             dma((2,)),
             dma((2,)),
             dma((2,)),

time: 16.8 us -> 16.4 us (0.976)
  the two profiles are of different devices: /device:TPU:1 before, /device:TPU:0 now
where the time goes in v2:
time: 16.4 us; the launch traced here: 16.3 us
  Pallas kernels  14.8 us (90%)
  other arithmetic  0.76 us (5%)
  between operations  0.69 us (4%)
    pallas_call x1, Pallas kernels, body(): pl.pallas_call(functools.partial(kernel, n), out_shape=pltpu.VMEM((rows_h...  14.8 us
    add x1, other arithmetic, body(): updated = iterate + precond[:, None] * residual  0.76 us

profile of v2, /device:TPU:0, one launch (start us, length us, event | category | flops | bytes accessed | tf_op | source)
XLA Modules:
  0.0 16.3 jit_solution(4365670477486562413)
XLA Ops:
  0.6 0.0 copy-start
  0.6 0.0 copy-start.1
  0.7 0.0 copy-start.2
  0.7 14.8 %shard_map.113 = f32[256,128]{1,0:T(8,128)S(1)} custom-call(f32[256,128]{1,0:T(8,128)} %iterate_hbm.1, f32[1,384,384]{2,1,0:T(8,128)} %schur_hbm.1, f32[256,256]{1,0:T(8,128)} %near_hbm.1, f32[16,32,256]{2,1,0:T(8,128)} %u_hbm.1, f32[16,32,256]{2,1,0:T(8,128)} %v_hbm.1, s32[1,16]{1,0:T(1,128)} %bitcast.3, s32[3,1,128]{2,1,0:T(1,128)} %bitcast.2, ...), custom_call_target="tpu_custom_call" | custom-call | tf_op jit(solution)/shard_map/pallas_call | solution.py:305
  15.5 0.0 copy-done
  15.5 0.0 copy-done.1
  15.5 0.0 copy-done.2
  15.5 0.8 %multiply_add_fusion = (f32[256,128]{1,0:T(8,128)}, f32[256,128]{1,0:T(8,128)}) fusion(f32[256,128]{1,0:T(8,128)S(1)} %copy-done, f32[256]{0:T(256)S(1)} %copy-done.2, f32[256,128]{1,0:T(8,128)S(1)} %copy-done.1, f32[256,128]{1,0:T(8,128)S(1)} %shard_map.113), kind=kLoop, calls=%fused_computation | loop fusion | flops 98304 | bytes 656384 | tf_op jit(solution)/shard_map/add | solution.py:340
Async XLA Ops:
  0.6 14.8 %copy-start = (f32[256,128]{1,0:T(8,128)S(1)}, f32[256,128]{1,0:T(8,128)}, u32[]{:S(2)}) copy-start(f32[256,128]{1,0:T(8,128)} %iterate_hbm.1) | copy-start | bytes 393220
  0.6 14.8 %copy-start.1 = (f32[256,128]{1,0:T(8,128)S(1)}, f32[256,128]{1,0:T(8,128)}, u32[]{:S(2)}) copy-start(f32[256,128]{1,0:T(8,128)} %param.11) | copy-start | bytes 393220
  0.7 14.8 %copy-start.2 = (f32[256]{0:T(256)S(1)}, f32[256]{0:T(256)}, u32[]{:S(2)}) copy-start(f32[256]{0:T(256)} %param.19) | copy-start | bytes 3076

commit v3 on v2

--- a/solution.py
+++ b/solution.py
@@ -76,7 +76,7 @@
     if STRIDE:
         groups = [[step + n // group * g for g in range(group - 1, -1, -1)] for step in range(n // group - 1, -1, -1)]
     else:
-        groups = [[first + g for g in range(group - 1, -1, -1)] for first in range(n - group, -1, -group)]
+        groups = [[first + g for g in range(group)] for first in range(n - group, -1, -group)]
     slot_of = {k: at for at, k in enumerate(k for members in groups for k in members)}
 
     names = {}
@@ -206,6 +206,30 @@
     mid = slice(face, 2 * face)
     b_both, b_high = pair(in_face[1])
     force = product(s_high[:, mid], s_low[:, mid], b_both, b_high)
+    @pl.when(has_above)
+    def _():
+        faces[0].wait_recv()
+
+    @pl.when(has_below)
+    def _():
+        faces[2].wait_recv()
+
+    for o in (0, 2):
+        span = slice(o * face, (o + 1) * face)
+        b_both, b_high = pair(in_face[o])
+        force = force + product(s_high[:, span], s_low[:, span], b_both, b_high)
+    out_force[0] = force[:face]
+    out_force[1] = force[2 * face :]
+    in_force[1] = force[mid]
+
+    @pl.when(has_above)
+    def _():
+        returns[0].start()
+
+    @pl.when(has_below)
+    def _():
+        returns[2].start()
+
     names["u"].wait()
     names["near"].wait()
     for at, members in enumerate(groups):
@@ -216,30 +240,6 @@
         u_low[:, span] = low
     near_high, near_low = halves(near[...])
     out_ref[...] = product(near_high, near_low, it_both, it_high)
-
-    @pl.when(has_above)
-    def _():
-        faces[0].wait_recv()
-
-    @pl.when(has_below)
-    def _():
-        faces[2].wait_recv()
-
-    for o in (0, 2):
-        span = slice(o * face, (o + 1) * face)
-        b_both, b_high = pair(in_face[o])
-        force = force + product(s_high[:, span], s_low[:, span], b_both, b_high)
-    out_force[0] = force[:face]
-    out_force[1] = force[2 * face :]
-    in_force[1] = force[mid]
-
-    @pl.when(has_above)
-    def _():
-        returns[0].start()
-
-    @pl.when(has_below)
-    def _():
-        returns[2].start()
 
     def far(first, size):
         for k, slot in slot_of.items():

time: 16.4 us -> 15.9 us (0.970)
  Pallas kernels: 14.8 us -> 14.3 us
    pallas_call x1, Pallas kernels: 14.8 us -> 14.3 us  [body(): pl.pallas_call(functools.partial(kernel, n), out_shape=pltpu.VMEM((rows_h...]
where the time goes in v3:
time: 15.9 us; the launch traced here: 15.7 us
  Pallas kernels  14.3 us (90%)
  other arithmetic  0.76 us (5%)
  between operations  0.69 us (4%)
    pallas_call x1, Pallas kernels, body(): pl.pallas_call(functools.partial(kernel, n), out_shape=pltpu.VMEM((rows_h...  14.3 us
    add x1, other arithmetic, body(): updated = iterate + precond[:, None] * residual  0.76 us

profile of v3, /device:TPU:0, one launch (start us, length us, event | category | flops | bytes accessed | tf_op | source)
XLA Modules:
  0.0 15.7 jit_solution(10317956371386345449)
XLA Ops:
  0.6 0.0 copy-start
  0.6 0.0 copy-start.1
  0.7 0.0 copy-start.2
  0.7 14.3 %shard_map.113 = f32[256,128]{1,0:T(8,128)S(1)} custom-call(f32[256,128]{1,0:T(8,128)} %iterate_hbm.1, f32[1,384,384]{2,1,0:T(8,128)} %schur_hbm.1, f32[256,256]{1,0:T(8,128)} %near_hbm.1, f32[16,32,256]{2,1,0:T(8,128)} %u_hbm.1, f32[16,32,256]{2,1,0:T(8,128)} %v_hbm.1, s32[1,16]{1,0:T(1,128)} %bitcast.3, s32[3,1,128]{2,1,0:T(1,128)} %bitcast.2, ...), custom_call_target="tpu_custom_call" | custom-call | tf_op jit(solution)/shard_map/pallas_call | solution.py:305
  14.9 0.0 copy-done
  15.0 0.0 copy-done.1
  15.0 0.0 copy-done.2
  15.0 0.8 %multiply_add_fusion = (f32[256,128]{1,0:T(8,128)}, f32[256,128]{1,0:T(8,128)}) fusion(f32[256,128]{1,0:T(8,128)S(1)} %copy-done, f32[256]{0:T(256)S(1)} %copy-done.2, f32[256,128]{1,0:T(8,128)S(1)} %copy-done.1, f32[256,128]{1,0:T(8,128)S(1)} %shard_map.113), kind=kLoop, calls=%fused_computation | loop fusion | flops 98304 | bytes 656384 | tf_op jit(solution)/shard_map/add | solution.py:340
Async XLA Ops:
  0.6 14.3 %copy-start = (f32[256,128]{1,0:T(8,128)S(1)}, f32[256,128]{1,0:T(8,128)}, u32[]{:S(2)}) copy-start(f32[256,128]{1,0:T(8,128)} %iterate_hbm.1) | copy-start | bytes 393220
  0.6 14.3 %copy-start.1 = (f32[256,128]{1,0:T(8,128)S(1)}, f32[256,128]{1,0:T(8,128)}, u32[]{:S(2)}) copy-start(f32[256,128]{1,0:T(8,128)} %param.11) | copy-start | bytes 393220
  0.7 14.3 %copy-start.2 = (f32[256]{0:T(256)S(1)}, f32[256]{0:T(256)}, u32[]{:S(2)}) copy-start(f32[256]{0:T(256)} %param.19) | copy-start | bytes 3076

commit v4 on v3

--- a/solution.py
+++ b/solution.py
@@ -76,7 +76,9 @@
     if STRIDE:
         groups = [[step + n // group * g for g in range(group - 1, -1, -1)] for step in range(n // group - 1, -1, -1)]
     else:
-        groups = [[first + g for g in range(group)] for first in range(n - group, -1, -group)]
+        halfway = n // 2 // group * group
+        firsts = [*range(halfway, n - group + 1, group), *range(halfway - group, -1, -group)]
+        groups = [[first + g for g in range(group)] for first in firsts]
     slot_of = {k: at for at, k in enumerate(k for members in groups for k in members)}
 
     names = {}

time: 15.9 us -> 15.6 us (0.981)
  the two profiles are of different devices: /device:TPU:0 before, /device:TPU:16 now
where the time goes in v4:
time: 15.6 us; the launch traced here: 15.5 us
  Pallas kernels  14 us (90%)
  other arithmetic  0.76 us (5%)
  between operations  0.69 us (4%)
    pallas_call x1, Pallas kernels, body(): pl.pallas_call(functools.partial(kernel, n), out_shape=pltpu.VMEM((rows_h...  14 us
    add x1, other arithmetic, body(): updated = iterate + precond[:, None] * residual  0.76 us

profile of v4, /device:TPU:16, one launch (start us, length us, event | category | flops | bytes accessed | tf_op | source)
XLA Modules:
  0.0 15.5 jit_solution(7687620342803679169)
XLA Ops:
  0.6 0.0 copy-start
  0.6 0.0 copy-start.1
  0.7 0.0 copy-start.2
  0.7 14.0 %shard_map.113 = f32[256,128]{1,0:T(8,128)S(1)} custom-call(f32[256,128]{1,0:T(8,128)} %iterate_hbm.1, f32[1,384,384]{2,1,0:T(8,128)} %schur_hbm.1, f32[256,256]{1,0:T(8,128)} %near_hbm.1, f32[16,32,256]{2,1,0:T(8,128)} %u_hbm.1, f32[16,32,256]{2,1,0:T(8,128)} %v_hbm.1, s32[1,16]{1,0:T(1,128)} %bitcast.3, s32[3,1,128]{2,1,0:T(1,128)} %bitcast.2, ...), custom_call_target="tpu_custom_call" | custom-call | tf_op jit(solution)/shard_map/pallas_call | solution.py:307
  14.7 0.0 copy-done
  14.7 0.0 copy-done.1
  14.7 0.0 copy-done.2
  14.7 0.8 %multiply_add_fusion = (f32[256,128]{1,0:T(8,128)}, f32[256,128]{1,0:T(8,128)}) fusion(f32[256,128]{1,0:T(8,128)S(1)} %copy-done, f32[256]{0:T(256)S(1)} %copy-done.2, f32[256,128]{1,0:T(8,128)S(1)} %copy-done.1, f32[256,128]{1,0:T(8,128)S(1)} %shard_map.113), kind=kLoop, calls=%fused_computation | loop fusion | flops 98304 | bytes 656384 | tf_op jit(solution)/shard_map/add | solution.py:342
Async XLA Ops:
  0.6 14.0 %copy-start = (f32[256,128]{1,0:T(8,128)S(1)}, f32[256,128]{1,0:T(8,128)}, u32[]{:S(2)}) copy-start(f32[256,128]{1,0:T(8,128)} %iterate_hbm.1) | copy-start | bytes 393220
  0.6 14.0 %copy-start.1 = (f32[256,128]{1,0:T(8,128)S(1)}, f32[256,128]{1,0:T(8,128)}, u32[]{:S(2)}) copy-start(f32[256,128]{1,0:T(8,128)} %param.11) | copy-start | bytes 393220
  0.7 14.0 %copy-start.2 = (f32[256]{0:T(256)S(1)}, f32[256]{0:T(256)}, u32[]{:S(2)}) copy-start(f32[256]{0:T(256)} %param.19) | copy-start | bytes 3076
